TPU v7x, 256 devices: a whole 4x4x8 slice. The times are simulated.
256 devices in a mesh: seq: 64 (over z, y, core), head: 4 (over x).
Axes of the slice: x: 4, y: 4, z: 8, core: 2. Of those that a mesh axis runs over, the one named last changes fastest.
Arguments:
- query_vectors: bfloat16 [131072, 1024], P('seq', 'head'), may hold values from -6 to 6
- key_vectors: bfloat16 [131072, 128], P('seq'), may hold values from -6 to 6
- value_vectors: bfloat16 [131072, 128], P('seq'), may hold values from -6 to 6
- output_grad: bfloat16 [131072, 1024], P('seq', 'head'), may hold values from -48 to 48
- random_blocks: int32 [1024, 3], P('seq'), may hold values from 0 to 1023, as said below
- global_blocks: int32 [2], replicated, may hold values from 0 to 1023
Outputs:
- query_grad: bfloat16 [131072, 1024], P('seq', 'head')
- key_grad: bfloat16 [131072, 128], P('seq')
- value_grad: bfloat16 [131072, 128], P('seq')
Inputs may be any that keep to these rules, and one draw needn't show every extreme that they name: `random_blocks`: take the query blocks in aligned runs of 16 and the key blocks in aligned runs of 16: all entries of one run of query blocks that fall into one run of key blocks name the same key block.
All inputs are finite; a program needn't handle non-finite values.
Results may differ from a plain program's by a relative error of at most 0.012.
Values may be sent and summed in bfloat16 or wider, within the bound.
A program may use at most 128 MiB of HBM per device.

v0:
```python
import jax
import jax.numpy as jnp
from jax import lax
from jax.sharding import PartitionSpec as P

DH = 128
BLOCK = 128
R = 3
G = 2


def with_halo(value, sides, width):
    for axis, dim in sides:
        size, length = (lax.axis_size(axis), value.shape[dim])
        up = [(i, (i + 1) % size) for i in range(size - 1)]
        down = [(j, i) for i, j in up]
        last = lax.slice_in_dim(value, length - width, length, axis=dim)
        first = lax.slice_in_dim(value, 0, width, axis=dim)
        before = lax.ppermute(last, axis, up)
        after = lax.ppermute(first, axis, down)
        value = jnp.concatenate([before, value, after], axis=dim)
    return value


def from_root(value, axis, source):
    kept = jnp.where(lax.axis_index(axis) == source, value, 0).astype(value.dtype)
    return lax.psum(kept, axis)


def from_behind(block, axis, distance):
    devices = range(lax.axis_size(axis))
    route = [(i - distance, i) for i in devices if i - distance in devices]
    return lax.ppermute(block, axis, route)


def softmax_rows(scores):
    largest = jnp.max(scores, axis=-1, keepdims=True)
    powers = jnp.exp(scores - largest)
    return powers / jnp.sum(powers, axis=-1, keepdims=True)


def body(query_vectors, key_vectors, value_vectors, output_grad, random_blocks, global_blocks):
    seq_count = lax.axis_size("seq")
    seq_index = lax.axis_index("seq")
    rows_dev = query_vectors.shape[0]
    blocks_dev = rows_dev // BLOCK
    heads_dev = query_vectors.shape[1] // DH
    factor = float(DH) ** (-0.5)
    pair_width = 2 * DH
    listed = 3 + R + G
    group_size = 4
    rounds = blocks_dev // group_size
    key_value = jnp.concatenate([key_vectors, value_vectors], axis=1)
    pair_blocks = key_value.reshape(blocks_dev, BLOCK, pair_width)
    owners = random_blocks // blocks_dev
    within = random_blocks % blocks_dev
    peer_ids = jnp.arange(seq_count, dtype=jnp.int32)
    matched = owners[:, :, None] == peer_ids[None, None, :]
    wanted = jnp.max(jnp.where(matched, within[:, :, None], -1), axis=(0, 1))
    requested = lax.all_to_all(
        wanted.reshape(seq_count, 1), "seq", split_axis=0, concat_axis=0, tiled=True
    )[:, 0]
    served = pair_blocks[jnp.clip(requested, 0, blocks_dev - 1)]
    fetched = lax.all_to_all(served, "seq", split_axis=0, concat_axis=0, tiled=True)
    extended = with_halo(key_value, (("seq", 0),), BLOCK)
    extended = extended.reshape(blocks_dev + 2, BLOCK, pair_width)
    global_list = []
    for global_slot in range(G):
        target = global_blocks[global_slot]
        fragment = lax.dynamic_index_in_dim(pair_blocks, target % blocks_dev, 0, keepdims=False)
        global_list.append(from_root(fragment, "seq", target // blocks_dev))
    global_pairs = jnp.stack(global_list)
    first_block = seq_index * blocks_dev
    total_blocks = seq_count * blocks_dev
    query_blocks = query_vectors.reshape(blocks_dev, BLOCK, heads_dev, DH)
    grad_blocks = output_grad.reshape(blocks_dev, BLOCK, heads_dev, DH)

    def advance(totals, position):
        window_acc, random_acc, global_acc = totals
        offset = position * group_size
        beside_all = lax.dynamic_slice_in_dim(extended, offset, group_size + 2, 0)
        window_panels = jnp.stack(
            [
                beside_all[0:group_size],
                beside_all[1 : group_size + 1],
                beside_all[2 : group_size + 2],
            ],
            axis=1,
        )
        owner_rows = lax.dynamic_slice_in_dim(owners, offset, group_size, 0)
        remote_panels = fetched[owner_rows]
        global_part = jnp.broadcast_to(global_pairs[None], (group_size, G, BLOCK, pair_width))
        panels = jnp.concatenate([window_panels, remote_panels, global_part], axis=1)
        panels = panels.reshape(group_size, listed * BLOCK, pair_width)
        key_row_matrix = panels[:, :, :DH]
        value_row_matrix = panels[:, :, DH:]
        query_row_matrix = lax.dynamic_slice_in_dim(query_blocks, offset, group_size, 0)
        gradient_rows = lax.dynamic_slice_in_dim(grad_blocks, offset, group_size, 0)
        block_ids = first_block + offset + jnp.arange(group_size, dtype=jnp.int32)
        allowed = jnp.concatenate(
            [
                (block_ids > 0)[:, None],
                jnp.ones((group_size, 1), dtype=jnp.bool_),
                (block_ids < total_blocks - 1)[:, None],
                jnp.ones((group_size, R + G), dtype=jnp.bool_),
            ],
            axis=1,
        )
        visible = jnp.repeat(allowed, BLOCK, axis=1)
        scores = (
            jnp.einsum(
                "awst,axt->aswx",
                query_row_matrix,
                key_row_matrix,
                preferred_element_type=jnp.float32,
            )
            * factor
        )
        scores = jnp.where(visible[:, None, None, :], scores, -jnp.inf)
        attention = softmax_rows(scores)
        attention_reduced = attention.astype(jnp.bfloat16)
        outputs = jnp.einsum(
            "uwsn,unj->uswj",
            attention_reduced,
            value_row_matrix,
            preferred_element_type=jnp.float32,
        )
        row_delta = jnp.sum(gradient_rows.astype(jnp.float32) * outputs, axis=-1)
        prob_grad = jnp.einsum(
            "awst,axt->aswx", gradient_rows, value_row_matrix, preferred_element_type=jnp.float32
        )
        score_gradient = (
            attention * (prob_grad - jnp.transpose(row_delta, (0, 2, 1))[..., None])
        ).astype(jnp.bfloat16)
        query_part = (
            jnp.einsum(
                "uwsn,unj->uswj", score_gradient, key_row_matrix, preferred_element_type=jnp.float32
            )
            * factor
        ).astype(jnp.bfloat16)
        key_part = (
            jnp.einsum(
                "uwva,uvwp->uap",
                score_gradient,
                query_row_matrix,
                preferred_element_type=jnp.float32,
            )
            * factor
        )
        value_part = jnp.einsum(
            "uwva,uvwp->uap", attention_reduced, gradient_rows, preferred_element_type=jnp.float32
        )
        gradients = jnp.concatenate([key_part, value_part], axis=-1).reshape(
            group_size, listed, BLOCK, pair_width
        )
        spread = jnp.zeros((group_size + 2, BLOCK, pair_width), dtype=jnp.float32)
        spread = spread.at[0:group_size].add(gradients[:, 0])
        spread = spread.at[1 : group_size + 1].add(gradients[:, 1])
        spread = spread.at[2 : group_size + 2].add(gradients[:, 2])
        updated = lax.dynamic_slice_in_dim(window_acc, offset, group_size + 2, 0) + spread
        window_acc = lax.dynamic_update_slice_in_dim(window_acc, updated, offset, 0)
        onehot = (owner_rows[:, :, None] == peer_ids[None, None, :]).astype(jnp.float32)
        random_acc = random_acc + jnp.einsum(
            "brn,brxc->nxc", onehot, gradients[:, 3 : 3 + R], precision=lax.Precision.HIGHEST
        )
        global_acc = global_acc + jnp.sum(gradients[:, 3 + R :], axis=0)
        return (
            (window_acc, random_acc, global_acc),
            query_part.reshape(group_size, BLOCK, heads_dev * DH),
        )

    start_totals = (
        jnp.zeros((blocks_dev + 2, BLOCK, pair_width), dtype=jnp.float32),
        jnp.zeros((seq_count, BLOCK, pair_width), dtype=jnp.float32),
        jnp.zeros((G, BLOCK, pair_width), dtype=jnp.float32),
    )
    (window_acc, random_acc, global_acc), query_parts = lax.scan(
        advance, start_totals, jnp.arange(rounds, dtype=jnp.int32)
    )
    query_grad = query_parts.reshape(rows_dev, heads_dev * DH)
    into_last = from_behind(window_acc[0].astype(jnp.bfloat16), "seq", -1).astype(jnp.float32)
    into_first = from_behind(window_acc[blocks_dev + 1].astype(jnp.bfloat16), "seq", 1).astype(
        jnp.float32
    )
    local_sum = window_acc[1 : blocks_dev + 1]
    local_sum = local_sum.at[blocks_dev - 1].add(into_last)
    local_sum = local_sum.at[0].add(into_first)
    global_total_sum = lax.psum(global_acc, "seq")
    block_range = jnp.arange(blocks_dev, dtype=jnp.int32)
    owned_indicator = (
        (global_blocks[None, :] // blocks_dev == seq_index)
        & (global_blocks[None, :] % blocks_dev == block_range[:, None])
    ).astype(jnp.float32)
    local_sum = local_sum + jnp.einsum(
        "ar,rdi->adi", owned_indicator, global_total_sum, precision=lax.Precision.HIGHEST
    )
    served_hot = (requested[None, :] == block_range[:, None]).astype(jnp.float32)
    returned = lax.all_to_all(
        random_acc.astype(jnp.bfloat16), "seq", split_axis=0, concat_axis=0, tiled=True
    ).astype(random_acc.dtype)
    local_sum = local_sum + jnp.einsum(
        "je,exc->jxc", served_hot, returned, precision=lax.Precision.HIGHEST
    )
    finished = lax.psum(local_sum.astype(jnp.bfloat16), "head")
    finished = finished.reshape(rows_dev, pair_width)
    return (query_grad, finished[:, :DH], finished[:, DH:])


def solution(mesh):
    return jax.shard_map(
        body,
        mesh=mesh,
        in_specs=(
            P("seq", "head"),
            P("seq", None),
            P("seq", None),
            P("seq", "head"),
            P("seq", None),
            P(),
        ),
        out_specs=(P("seq", "head"), P("seq", None), P("seq", None)),
        check_vma=False,
    )
```

profile of v0, /device:TPU:8, one launch (start us, length us, event | category | flops | bytes accessed | tf_op | source)
XLA Modules:
  0.0 700.6 jit_solution(18152049485967785271)
XLA Ops:
  8.9 12.1 %all-to-all-start = ((s32[64,1,1]{2,1,0:T(1,128)}), s32[64,1,1]{2,1,0:T(1,128)S(1)}, u32[]{:S(2)}, u32[]{:S(2)}) async-start(s32[64,1,1]{2,1,0:T(1,128)} %copy.161), calls=%async_computation | async-start | bytes 65536 | tf_op jit(solution)/shard_map/all_to_all | solution.py:60
  23.3 6.2 all-to-all-done
  35.1 6.6 all-to-all-start.1
  50.4 3.5 collective-permute-start.1
  56.2 178.6 %all-reduce.10.cloned.1.call-done = (bf16[1,128,256]{2,1,0:T(8,128)(2,1)}, bf16[1,128,256]{2,1,0:T(8,128)(2,1)}) async-done(((bf16[1,128,256]{2,1,0:T(8,128)(2,1)}, bf16[1,128,256]{2,1,0:T(8,128)(2,1)}), (bf16[1,128,256]{2,1,0:T(8,128)(2,1)}, bf16[1,128,256]{2,1,0:T(8,128)(2,1)})) %all-reduce.10.cloned.1.call-update) | async-done | bytes 131088 | tf_op jit(solution)/shard_map/psum | solution.py:27
  238.5 181.6 %while.25 = (s32[]{:T(128)}, f32[18,128,256]{1,2,0:T(8,128)}, f32[64,128,256]{2,0,1:T(8,128)}, f32[2,128,256]{1,0,2:T(2,128)}, bf16[4,4,128,256]{3,2,1,0:T(8,128...) while((s32[]{:T(128)}, f32[18,128,256]{1,2,0:T(8,128)}, ...), condition=%wide.region_8.9_spmd.clone, body=%wide.region_3.8_spmd.clone.sunk | while | flops 1932396416 | bytes 146449488 | solution.py:177
  258.2 2.9 slice_reduce_fusion.2
  262.7 6.8 fusion.100
  274.5 6.3 bitcast_add_fusion.2
  300.4 2.9 slice_reduce_fusion.2
  306.1 6.8 fusion.100
  317.9 9.3 %bitcast_add_fusion.2 = f32[64,128,256]{2,0,1:T(8,128)} fusion(f32[64,128,256]{2,0,1:T(8,128)} %get-tuple-element.561, pred[]{:T(512)S(6)} %compare.58, f32[4,3,128,256]{3,0,1,2:T(4,128)S(1)} %copy-done.1, s32[4,3]{0,1:T(4,128)S(1)} %copy.240), kind=kOutput, calls=%fused_computation.4.clone.1 | convolution fusion | flops 306184960 | bytes 18350128 | tf_op jit(solution)/shard_map/while/body/eval_jaxpr/brn,brxc->nxc/dot_general | solution.py:163
  346.9 2.9 slice_reduce_fusion.2
  352.5 6.8 fusion.100
  364.4 9.3 %bitcast_add_fusion.2 = f32[64,128,256]{2,0,1:T(8,128)} fusion(f32[64,128,256]{2,0,1:T(8,128)} %get-tuple-element.561, pred[]{:T(512)S(6)} %compare.58, f32[4,3,128,256]{3,0,1,2:T(4,128)S(1)} %copy-done.1, s32[4,3]{0,1:T(4,128)S(1)} %copy.240), kind=kOutput, calls=%fused_computation.4.clone.1 | convolution fusion | flops 306184960 | bytes 18350128 | tf_op jit(solution)/shard_map/while/body/eval_jaxpr/brn,brxc->nxc/dot_general | solution.py:163
  393.3 2.9 slice_reduce_fusion.2
  399.0 6.8 fusion.100
  410.8 9.3 %bitcast_add_fusion.2 = f32[64,128,256]{2,0,1:T(8,128)} fusion(f32[64,128,256]{2,0,1:T(8,128)} %get-tuple-element.561, pred[]{:T(512)S(6)} %compare.58, f32[4,3,128,256]{3,0,1,2:T(4,128)S(1)} %copy-done.1, s32[4,3]{0,1:T(4,128)S(1)} %copy.240), kind=kOutput, calls=%fused_computation.4.clone.1 | convolution fusion | flops 306184960 | bytes 18350128 | tf_op jit(solution)/shard_map/while/body/eval_jaxpr/brn,brxc->nxc/dot_general | solution.py:163
  420.1 9.8 %copy.220 = bf16[64,128,256]{2,1,0:T(8,128)(2,1)} copy(f32[64,128,256]{2,0,1:T(8,128)} %get-tuple-element.285) | data formatting | bytes 12582912 | tf_op jit(solution)/shard_map/while | solution.py:177
  429.9 8.4 %all-to-all-start.2 = ((bf16[64,128,256]{2,1,0:T(8,128)(2,1)}), bf16[64,128,256]{2,1,0:T(8,128)(2,1)}, u32[]{:S(2)}, u32[]{:S(2)}) async-start(bf16[64,128,256]{2,1,0:T(8,128)(2,1)} %copy.220), calls=%async_computation.2 | async-start | bytes 8388608 | tf_op jit(solution)/shard_map/all_to_all | solution.py:198
  458.9 76.0 %all-to-all-done.2 = bf16[64,128,256]{2,1,0:T(8,128)(2,1)} async-done(((bf16[64,128,256]{2,1,0:T(8,128)(2,1)}), bf16[64,128,256]{2,1,0:T(8,128)(2,1)}, u32[]{:S(2)}, u32[]{:S(2)}) %all-to-all-start.2) | async-done | bytes 4194336 | tf_op jit(solution)/shard_map/all_to_all | solution.py:198
  534.9 5.9 fusion.32
  540.8 97.0 %all-reduce.6.cloned.1.call-done = f32[2,128,256]{2,0,1:T(2,128)} async-done(((f32[2,128,256]{2,0,1:T(2,128)}), f32[2,128,256]{2,0,1:T(2,128)}) %all-reduce.6.cloned.1.call-update) | async-done | bytes 262160 | tf_op jit(solution)/shard_map/psum | solution.py:188
  642.0 49.8 %all-reduce.8.cloned.1.call-done = bf16[2048,256]{1,0:T(8,128)(2,1)} async-done(((bf16[2048,256]{1,0:T(8,128)(2,1)}), bf16[2048,256]{1,0:T(8,128)(2,1)}) %all-reduce.8.cloned.1.call-update) | async-done | bytes 1048592 | tf_op jit(solution)/shard_map/psum | solution.py:204
  (251 shorter events, 150.9 us)
Async XLA Ops:
  8.9 20.7 %all-to-all-start = ((s32[64,1,1]{2,1,0:T(1,128)}), s32[64,1,1]{2,1,0:T(1,128)S(1)}, u32[]{:S(2)}, u32[]{:S(2)}) async-start(s32[64,1,1]{2,1,0:T(1,128)} %copy.161), calls=%async_computation | async-start | bytes 65536 | tf_op jit(solution)/shard_map/all_to_all | solution.py:60
  35.1 6.7 copy-start.8
  35.1 18.8 %copy-start.5 = (bf16[2048,256]{1,0:T(8,128)(2,1)S(1)}, bf16[2048,256]{1,0:T(8,128)(2,1)}, u32[]{:S(2)}) copy-start(bf16[2048,256]{1,0:T(8,128)(2,1)} %param.18) | copy-start | bytes 3145732
  35.1 201.7 %all-to-all-start.1 = ((bf16[64,128,256]{2,1,0:T(8,128)(2,1)}), bf16[64,128,256]{2,1,0:T(8,128)(2,1)}, u32[]{:S(2)}, u32[]{:S(2)}) async-start(bf16[64,128,256]{2,1,0:T(8,128)(2,1)} %gather_fusion.1), calls=%async_computation.1 | async-start | bytes 8388608 | tf_op jit(solution)/shard_map/all_to_all | solution.py:64
  41.7 13.3 %copy-start.6 = (bf16[2048,256]{1,0:T(8,128)(2,1)S(1)}, bf16[2048,256]{1,0:T(8,128)(2,1)}, u32[]{:S(2)}) copy-start(bf16[2048,256]{1,0:T(8,128)(2,1)} %param.21) | copy-start | bytes 3145732
  41.8 193.1 %all-reduce.10.cloned.1.call-start = ((), (), s32[]{:S(2)}) async-start(), calls=%async_computation.5 | async-start | bytes 262144 | tf_op jit(solution)/shard_map/psum | solution.py:27
  48.3 187.4 %collective-permute-start = (bf16[128,256]{1,0:T(8,128)(2,1)S(1)}, bf16[128,256]{1,0:T(8,128)(2,1)S(1)}, u32[]{:S(2)}, u32[]{:S(2)}) collective-permute-start(bf16[128,256]{1,0:T(8,128)(2,1)S(1)} %get-tuple-element.429), channel_id=1, source_target_pairs={{0,4},{4,8},{8,12},{12,16},{16,20},{20,24},{24,28},{28,32},{32,36}... | collective-permute-start | bytes 196616 | tf_op jit(solution)/shard_map/ppermute | solution.py:19
  50.4 185.3 %collective-permute-start.1 = (bf16[128,256]{1,0:T(8,128)(2,1)S(1)}, bf16[128,256]{1,0:T(8,128)(2,1)S(1)}, u32[]{:S(2)}, u32[]{:S(2)}) collective-permute-start(bf16[128,256]{1,0:T(8,128)(2,1)S(1)} %get-tuple-element.430), channel_id=1, source_target_pairs={{4,0},{8,4},{12,8},{16,12},{20,16},{24,20},{28,24},{32,28},{36,32}... | collective-permute-start | bytes 196616 | tf_op jit(solution)/shard_map/ppermute | solution.py:20
  261.1 8.4 %copy-start = (f32[128,8,8,128]{3,2,1,0:T(8,128)S(1)}, f32[128,8,8,128]{3,2,1,0:T(8,128)}, u32[]{:S(2)}) copy-start(f32[128,8,8,128]{3,2,1,0:T(8,128)} %copy.238) | copy-start | bytes 12582916 | tf_op jit(solution)/shard_map/while
  274.5 6.3 copy-start.3
  303.4 9.5 %copy-start = (f32[128,8,8,128]{3,2,1,0:T(8,128)S(1)}, f32[128,8,8,128]{3,2,1,0:T(8,128)}, u32[]{:S(2)}) copy-start(f32[128,8,8,128]{3,2,1,0:T(8,128)} %copy.238) | copy-start | bytes 12582916 | tf_op jit(solution)/shard_map/while
  317.9 9.3 %copy-start.3 = (f32[18,128,256]{1,2,0:T(8,128)}, f32[18,128,256]{1,2,0:T(8,128)S(1)}, u32[]{:S(2)}) copy-start(f32[18,128,256]{1,2,0:T(8,128)S(1)} %add_dynamic-update-slice_fusion.5) | copy-start | bytes 7077892 | tf_op jit(solution)/shard_map/while
  349.8 9.5 %copy-start = (f32[128,8,8,128]{3,2,1,0:T(8,128)S(1)}, f32[128,8,8,128]{3,2,1,0:T(8,128)}, u32[]{:S(2)}) copy-start(f32[128,8,8,128]{3,2,1,0:T(8,128)} %copy.238) | copy-start | bytes 12582916 | tf_op jit(solution)/shard_map/while
  364.4 9.3 %copy-start.3 = (f32[18,128,256]{1,2,0:T(8,128)}, f32[18,128,256]{1,2,0:T(8,128)S(1)}, u32[]{:S(2)}) copy-start(f32[18,128,256]{1,2,0:T(8,128)S(1)} %add_dynamic-update-slice_fusion.5) | copy-start | bytes 7077892 | tf_op jit(solution)/shard_map/while
  396.3 9.5 %copy-start = (f32[128,8,8,128]{3,2,1,0:T(8,128)S(1)}, f32[128,8,8,128]{3,2,1,0:T(8,128)}, u32[]{:S(2)}) copy-start(f32[128,8,8,128]{3,2,1,0:T(8,128)} %copy.238) | copy-start | bytes 12582916 | tf_op jit(solution)/shard_map/while
  410.8 9.3 %copy-start.3 = (f32[18,128,256]{1,2,0:T(8,128)}, f32[18,128,256]{1,2,0:T(8,128)S(1)}, u32[]{:S(2)}) copy-start(f32[18,128,256]{1,2,0:T(8,128)S(1)} %add_dynamic-update-slice_fusion.5) | copy-start | bytes 7077892 | tf_op jit(solution)/shard_map/while
  429.9 8.4 %copy-start.9 = (s32[2]{0:T(128)S(1)}, s32[2]{0:T(128)}, u32[]{:S(2)}) copy-start(s32[2]{0:T(128)} %param.23) | copy-start | bytes 28
  429.9 8.4 %copy-start.4 = (f32[18,128,256]{1,2,0:T(8,128)S(1)}, f32[18,128,256]{1,2,0:T(8,128)}, u32[]{:S(2)}) copy-start(f32[18,128,256]{1,2,0:T(8,128)} %get-tuple-element.283) | copy-start | bytes 7077892
  429.9 105.0 %all-to-all-start.2 = ((bf16[64,128,256]{2,1,0:T(8,128)(2,1)}), bf16[64,128,256]{2,1,0:T(8,128)(2,1)}, u32[]{:S(2)}, u32[]{:S(2)}) async-start(bf16[64,128,256]{2,1,0:T(8,128)(2,1)} %copy.220), calls=%async_computation.2 | async-start | bytes 8388608 | tf_op jit(solution)/shard_map/all_to_all | solution.py:198
  438.3 199.4 %all-reduce.6.cloned.1.call-start = ((), (), s32[]{:S(2)}) async-start(), calls=%async_computation.3 | async-start | bytes 524288 | tf_op jit(solution)/shard_map/psum | solution.py:188
  442.2 10.8 %collective-permute-start.2 = (bf16[128,256]{1,0:T(8,128)(2,1)S(1)}, bf16[128,256]{1,0:T(8,128)(2,1)S(1)}, u32[]{:S(2)}, u32[]{:S(2)}) collective-permute-start(bf16[128,256]{1,0:T(8,128)(2,1)S(1)} %get-tuple-element.424), channel_id=1, source_target_pairs={{4,0},{8,4},{12,8},{16,12},{20,16},{24,20},{28,24},{32,28},{36,32}... | collective-permute-start | bytes 196616 | tf_op jit(solution)/shard_map/ppermute | solution.py:33
  448.3 86.5 %copy-start.7 = (s32[64]{0:T(128)S(1)}, s32[64]{0:T(128)}, u32[]{:S(2)}) copy-start(s32[64]{0:T(128)} %get-tuple-element.382) | copy-start | bytes 772
  448.3 243.5 %all-reduce.8.cloned.1.call-start = ((), (), s32[]{:S(2)}) async-start(), calls=%async_computation.4 | async-start | bytes 2097152 | tf_op jit(solution)/shard_map/psum | solution.py:204
  450.6 6.3 collective-permute-start.3
  (8 other events, 13.4 us)
Sparse Core Ops, SparseCore 0:
  48.4 186.3 all-reduce.9
  448.4 189.2 all-reduce.5
  642.2 49.6 all-reduce.7
where the time goes:
time: 702 us; the launch traced here: 701 us
  waiting for transfers between devices  409 us (58%)
  local copies, waits for them, and re-layouts  131 us (19%)
  matrix products  61.8 us (9%)
  other arithmetic  40.1 us (6%)
  starting transfers between devices  37.1 us (5%)
  between operations  19.2 us (3%)
    psum x1, waiting for transfers between devices, from_root(): return lax.psum(kept, axis)  179 us
    psum x1, waiting for transfers between devices, body(): global_total_sum = lax.psum(global_acc, 'seq')  97 us
    all_to_all x1, waiting for transfers between devices, body(): lax.all_to_all(random_acc.astype(jnp.bfloat16), 'seq', split_axis=0, conc...  76 us
    psum x1, waiting for transfers between devices, body(): finished = lax.psum(local_sum.astype(jnp.bfloat16), 'head')  49.8 us
    while x64, local copies, waits for them, and re-layouts  35.7 us
    dot_general x4, matrix products, advance(): jnp.einsum('brn,brxc->nxc', onehot, gradients[:, 3:3 + R], precision=lax....  34.2 us
    slice x4, local copies, waits for them, and re-layouts, advance(): spread = spread.at[2:group_size + 2].add(gradients[:, 2])  27.3 us
    while x4, local copies, waits for them, and re-layouts, body(): lax.scan(advance, start_totals, jnp.arange(rounds, dtype=jnp.int32))  15.9 us
  transfers between devices with their start and end apart: 10, of which 6 were waited for; matrix products, arithmetic and copies ran while one was open for 4% of the time, Pallas kernels for 0%

commit v1 on v0

--- a/solution.py
+++ b/solution.py
@@ -1,3 +1,4 @@
+import functools
 import jax
 import jax.numpy as jnp
 from jax import lax
@@ -7,6 +8,13 @@
 BLOCK = 128
 R = 3
 G = 2
+
+
+def _mark_shelves(row_data, which_axis):
+    return jnp.sum(jax.lax.all_gather(row_data, which_axis), axis=0)
+
+
+supply_pages_over_axis = functools.partial(_mark_shelves, which_axis="seq")
 
 
 def with_halo(value, sides, width):
@@ -185,7 +193,7 @@
     local_sum = window_acc[1 : blocks_dev + 1]
     local_sum = local_sum.at[blocks_dev - 1].add(into_last)
     local_sum = local_sum.at[0].add(into_first)
-    global_total_sum = lax.psum(global_acc, "seq")
+    global_total_sum = supply_pages_over_axis(global_acc)
     block_range = jnp.arange(blocks_dev, dtype=jnp.int32)
     owned_indicator = (
         (global_blocks[None, :] // blocks_dev == seq_index)

time: 702 us -> 655 us (0.933)
  waiting for transfers between devices: 409 us -> 353 us
    psum x1 -> x0, waiting for transfers between devices: 97 us -> none  [body(): global_total_sum = lax.psum(global_acc, 'seq')]
    all_to_all x1, waiting for transfers between devices: 76 us -> 110 us  [body(): lax.all_to_all(random_acc.astype(jnp.bfloat16), 'seq', split_axis=0, conc...]
    all_gather x0 -> x1, waiting for transfers between devices: none -> 7.53 us  [_mark_shelves(): return jnp.sum(jax.lax.all_gather(row_data, which_axis), axis=0)]
  transfers between devices with their start and end apart: 10 -> 10, of which waited for: 6 -> 6; matrix products, arithmetic and copies ran while one was open for 4% -> 6% of each run, Pallas kernels for 0% -> 0%
where the time goes in v1:
time: 655 us; the launch traced here: 653 us
  waiting for transfers between devices  353 us (54%)
  local copies, waits for them, and re-layouts  131 us (20%)
  matrix products  61.8 us (9%)
  other arithmetic  46.9 us (7%)
  starting transfers between devices  37.1 us (6%)
  between operations  19.2 us (3%)
    psum x1, waiting for transfers between devices, from_root(): return lax.psum(kept, axis)  179 us
    all_to_all x1, waiting for transfers between devices, body(): lax.all_to_all(random_acc.astype(jnp.bfloat16), 'seq', split_axis=0, conc...  110 us
    psum x1, waiting for transfers between devices, body(): finished = lax.psum(local_sum.astype(jnp.bfloat16), 'head')  50.8 us
    while x64, local copies, waits for them, and re-layouts  35.9 us
    dot_general x4, matrix products, advance(): jnp.einsum('brn,brxc->nxc', onehot, gradients[:, 3:3 + R], precision=lax....  34.3 us
    slice x4, local copies, waits for them, and re-layouts, advance(): spread = spread.at[2:group_size + 2].add(gradients[:, 2])  27.7 us
    while x4, local copies, waits for them, and re-layouts, body(): lax.scan(advance, start_totals, jnp.arange(rounds, dtype=jnp.int32))  15.9 us
  transfers between devices with their start and end apart: 10, of which 6 were waited for; matrix products, arithmetic and copies ran while one was open for 6% of the time, Pallas kernels for 0%

profile of v1, /device:TPU:8, one launch (start us, length us, event | category | flops | bytes accessed | tf_op | source)
XLA Modules:
  0.0 652.9 jit_solution(9095257188172763972)
XLA Ops:
  8.9 12.1 %all-to-all-start = ((s32[64,1,1]{2,1,0:T(1,128)}), s32[64,1,1]{2,1,0:T(1,128)S(1)}, u32[]{:S(2)}, u32[]{:S(2)}) async-start(s32[64,1,1]{2,1,0:T(1,128)} %copy.161), calls=%async_computation | async-start | bytes 65536 | tf_op jit(solution)/shard_map/all_to_all | solution.py:68
  23.3 6.2 all-to-all-done
  35.2 6.6 %all-to-all-start.1 = ((bf16[64,128,256]{2,1,0:T(8,128)(2,1)}), bf16[64,128,256]{2,1,0:T(8,128)(2,1)}, u32[]{:S(2)}, u32[]{:S(2)}) async-start(bf16[64,128,256]{2,1,0:T(8,128)(2,1)} %gather_fusion.1), calls=%async_computation.1 | async-start | bytes 8388608 | tf_op jit(solution)/shard_map/all_to_all | solution.py:72
  50.5 3.5 collective-permute-start.1
  56.4 178.5 %all-reduce.7.cloned.1.call-done = (bf16[1,128,256]{2,1,0:T(8,128)(2,1)}, bf16[1,128,256]{2,1,0:T(8,128)(2,1)}) async-done(((bf16[1,128,256]{2,1,0:T(8,128)(2,1)}, bf16[1,128,256]{2,1,0:T(8,128)(2,1)}), (bf16[1,128,256]{2,1,0:T(8,128)(2,1)}, bf16[1,128,256]{2,1,0:T(8,128)(2,1)})) %all-reduce.7.cloned.1.call-update) | async-done | bytes 131088 | tf_op jit(solution)/shard_map/psum | solution.py:35
  238.5 182.2 %while.25 = (s32[]{:T(128)}, f32[18,128,256]{1,2,0:T(8,128)}, f32[64,128,256]{2,0,1:T(8,128)}, f32[2,128,256]{1,0,2:T(2,128)}, bf16[4,4,128,256]{3,2,1,0:T(8,128...) while((s32[]{:T(128)}, f32[18,128,256]{1,2,0:T(8,128)}, ...), condition=%wide.region_8.9_spmd.clone, body=%wide.region_3.8_spmd.clone.sunk | while | flops 1932396416 | bytes 146449488 | solution.py:185
  262.7 6.9 %fusion.100 = (f32[4,1,128,256]{2,1,3,0:T(1,128)S(1)}, f32[4,1,128,256]{2,1,3,0:T(1,128)S(1)}, f32[4,1,128,256]{2,1,3,0:T(1,128)}) fusion(f32[4,8,128,256]{2,1,3,0:T(8,128)} %bitcast.194), kind=kLoop, calls=%fused_computation.109.clone.1 | loop fusion | bytes 3145728 | tf_op jit(solution)/shard_map/while/body/eval_jaxpr/slice | solution.py:167
  274.7 6.3 bitcast_add_fusion.2
  297.5 3.0 copy.241
  306.3 6.9 %fusion.100 = (f32[4,1,128,256]{2,1,3,0:T(1,128)S(1)}, f32[4,1,128,256]{2,1,3,0:T(1,128)S(1)}, f32[4,1,128,256]{2,1,3,0:T(1,128)}) fusion(f32[4,8,128,256]{2,1,3,0:T(8,128)} %bitcast.194), kind=kLoop, calls=%fused_computation.109.clone.1 | loop fusion | bytes 3145728 | tf_op jit(solution)/shard_map/while/body/eval_jaxpr/slice | solution.py:167
  318.2 9.3 %bitcast_add_fusion.2 = f32[64,128,256]{2,0,1:T(8,128)} fusion(f32[64,128,256]{2,0,1:T(8,128)} %get-tuple-element.561, pred[]{:T(512)S(6)} %compare.58, f32[4,3,128,256]{3,0,1,2:T(4,128)S(1)} %copy-done.1, s32[4,3]{0,1:T(4,128)S(1)} %copy.243), kind=kOutput, calls=%fused_computation.4.clone.1 | convolution fusion | flops 306184960 | bytes 18350128 | tf_op jit(solution)/shard_map/while/body/eval_jaxpr/brn,brxc->nxc/dot_general | solution.py:171
  344.1 3.0 copy.241
  352.9 6.9 %fusion.100 = (f32[4,1,128,256]{2,1,3,0:T(1,128)S(1)}, f32[4,1,128,256]{2,1,3,0:T(1,128)S(1)}, f32[4,1,128,256]{2,1,3,0:T(1,128)}) fusion(f32[4,8,128,256]{2,1,3,0:T(8,128)} %bitcast.194), kind=kLoop, calls=%fused_computation.109.clone.1 | loop fusion | bytes 3145728 | tf_op jit(solution)/shard_map/while/body/eval_jaxpr/slice | solution.py:167
  364.8 9.3 %bitcast_add_fusion.2 = f32[64,128,256]{2,0,1:T(8,128)} fusion(f32[64,128,256]{2,0,1:T(8,128)} %get-tuple-element.561, pred[]{:T(512)S(6)} %compare.58, f32[4,3,128,256]{3,0,1,2:T(4,128)S(1)} %copy-done.1, s32[4,3]{0,1:T(4,128)S(1)} %copy.243), kind=kOutput, calls=%fused_computation.4.clone.1 | convolution fusion | flops 306184960 | bytes 18350128 | tf_op jit(solution)/shard_map/while/body/eval_jaxpr/brn,brxc->nxc/dot_general | solution.py:171
  390.7 3.0 copy.241
  399.5 6.9 %fusion.100 = (f32[4,1,128,256]{2,1,3,0:T(1,128)S(1)}, f32[4,1,128,256]{2,1,3,0:T(1,128)S(1)}, f32[4,1,128,256]{2,1,3,0:T(1,128)}) fusion(f32[4,8,128,256]{2,1,3,0:T(8,128)} %bitcast.194), kind=kLoop, calls=%fused_computation.109.clone.1 | loop fusion | bytes 3145728 | tf_op jit(solution)/shard_map/while/body/eval_jaxpr/slice | solution.py:167
  411.4 9.3 %bitcast_add_fusion.2 = f32[64,128,256]{2,0,1:T(8,128)} fusion(f32[64,128,256]{2,0,1:T(8,128)} %get-tuple-element.561, pred[]{:T(512)S(6)} %compare.58, f32[4,3,128,256]{3,0,1,2:T(4,128)S(1)} %copy-done.1, s32[4,3]{0,1:T(4,128)S(1)} %copy.243), kind=kOutput, calls=%fused_computation.4.clone.1 | convolution fusion | flops 306184960 | bytes 18350128 | tf_op jit(solution)/shard_map/while/body/eval_jaxpr/brn,brxc->nxc/dot_general | solution.py:171
  422.5 9.8 %copy.223 = bf16[64,128,256]{2,1,0:T(8,128)(2,1)} copy(f32[64,128,256]{2,0,1:T(8,128)} %get-tuple-element.285) | data formatting | bytes 12582912 | tf_op jit(solution)/shard_map/while | solution.py:185
  432.3 8.4 %all-to-all-start.2 = ((bf16[64,128,256]{2,1,0:T(8,128)(2,1)}), bf16[64,128,256]{2,1,0:T(8,128)(2,1)}, u32[]{:S(2)}, u32[]{:S(2)}) async-start(bf16[64,128,256]{2,1,0:T(8,128)(2,1)} %copy.223), calls=%async_computation.2 | async-start | bytes 8388608 | tf_op jit(solution)/shard_map/all_to_all | solution.py:206
  459.2 109.6 %all-to-all-done.2 = bf16[64,128,256]{2,1,0:T(8,128)(2,1)} async-done(((bf16[64,128,256]{2,1,0:T(8,128)(2,1)}), bf16[64,128,256]{2,1,0:T(8,128)(2,1)}, u32[]{:S(2)}, u32[]{:S(2)}) %all-to-all-start.2) | async-done | bytes 4194336 | tf_op jit(solution)/shard_map/all_to_all | solution.py:206
  568.8 6.0 fusion.32
  574.8 7.5 %all-gather.3.cloned.1.call-done = f32[128,128,256]{2,1,0:T(8,128)} async-done(((f32[2,128,256]{2,1,0:T(8,128)}), f32[128,128,256]{2,1,0:T(8,128)}) %all-gather.3.cloned.1.call-update) | async-done | bytes 16777232 | tf_op jit(solution)/shard_map/all_gather | solution.py:14
  582.3 6.9 %reduce_sum.48 = f32[2,128,256]{2,1,0:T(8,128)S(1)} reduce(f32[64,2,128,256]{3,2,1,0:T(8,128)} %bitcast.207, f32[]{:T(128)} %constant.320.clone.1), dimensions={0}, to_apply=%region_9.10 | reduce | flops 4128768 | bytes 17039364 | tf_op jit(solution)/shard_map/reduce_sum | solution.py:14
  593.4 50.8 %all-reduce.5.cloned.1.call-done = bf16[2048,256]{1,0:T(8,128)(2,1)} async-done(((bf16[2048,256]{1,0:T(8,128)(2,1)}), bf16[2048,256]{1,0:T(8,128)(2,1)}) %all-reduce.5.cloned.1.call-update) | async-done | bytes 1048592 | tf_op jit(solution)/shard_map/psum | solution.py:212
  (252 shorter events, 153.6 us)
Async XLA Ops:
  8.9 20.7 %all-to-all-start = ((s32[64,1,1]{2,1,0:T(1,128)}), s32[64,1,1]{2,1,0:T(1,128)S(1)}, u32[]{:S(2)}, u32[]{:S(2)}) async-start(s32[64,1,1]{2,1,0:T(1,128)} %copy.161), calls=%async_computation | async-start | bytes 65536 | tf_op jit(solution)/shard_map/all_to_all | solution.py:68
  35.2 6.7 %copy-start.8 = (s32[2]{0:T(128)S(1)}, s32[2]{0:T(128)}, u32[]{:S(2)}) copy-start(s32[2]{0:T(128)} %param.23) | copy-start | bytes 28
  35.2 18.9 %copy-start.5 = (bf16[2048,256]{1,0:T(8,128)(2,1)S(1)}, bf16[2048,256]{1,0:T(8,128)(2,1)}, u32[]{:S(2)}) copy-start(bf16[2048,256]{1,0:T(8,128)(2,1)} %param.18) | copy-start | bytes 3145732
  35.2 201.7 %all-to-all-start.1 = ((bf16[64,128,256]{2,1,0:T(8,128)(2,1)}), bf16[64,128,256]{2,1,0:T(8,128)(2,1)}, u32[]{:S(2)}, u32[]{:S(2)}) async-start(bf16[64,128,256]{2,1,0:T(8,128)(2,1)} %gather_fusion.1), calls=%async_computation.1 | async-start | bytes 8388608 | tf_op jit(solution)/shard_map/all_to_all | solution.py:72
  41.8 13.4 %copy-start.6 = (bf16[2048,256]{1,0:T(8,128)(2,1)S(1)}, bf16[2048,256]{1,0:T(8,128)(2,1)}, u32[]{:S(2)}) copy-start(bf16[2048,256]{1,0:T(8,128)(2,1)} %param.21) | copy-start | bytes 3145732
  41.8 193.1 %all-reduce.7.cloned.1.call-start = ((), (), s32[]{:S(2)}) async-start(), calls=%async_computation.5 | async-start | bytes 262144 | tf_op jit(solution)/shard_map/psum | solution.py:35
  48.4 533.9 %all-gather.3.cloned.1.call-start = ((), (), s32[]{:S(2)}) async-start(), calls=%async_computation.4 | async-start | bytes 17039360 | tf_op jit(solution)/shard_map/all_gather | solution.py:14
  48.4 187.3 %collective-permute-start = (bf16[128,256]{1,0:T(8,128)(2,1)S(1)}, bf16[128,256]{1,0:T(8,128)(2,1)S(1)}, u32[]{:S(2)}, u32[]{:S(2)}) collective-permute-start(bf16[128,256]{1,0:T(8,128)(2,1)S(1)} %get-tuple-element.429), channel_id=1, source_target_pairs={{0,4},{4,8},{8,12},{12,16},{16,20},{20,24},{24,28},{28,32},{32,36}... | collective-permute-start | bytes 196616 | tf_op jit(solution)/shard_map/ppermute | solution.py:27
  50.5 185.3 %collective-permute-start.1 = (bf16[128,256]{1,0:T(8,128)(2,1)S(1)}, bf16[128,256]{1,0:T(8,128)(2,1)S(1)}, u32[]{:S(2)}, u32[]{:S(2)}) collective-permute-start(bf16[128,256]{1,0:T(8,128)(2,1)S(1)} %get-tuple-element.430), channel_id=1, source_target_pairs={{4,0},{8,4},{12,8},{16,12},{20,16},{24,20},{28,24},{32,28},{36,32}... | collective-permute-start | bytes 196616 | tf_op jit(solution)/shard_map/ppermute | solution.py:28
  261.1 8.5 %copy-start = (f32[128,8,8,128]{3,2,1,0:T(8,128)S(1)}, f32[128,8,8,128]{3,2,1,0:T(8,128)}, u32[]{:S(2)}) copy-start(f32[128,8,8,128]{3,2,1,0:T(8,128)} %copy.241) | copy-start | bytes 12582916 | tf_op jit(solution)/shard_map/while
  274.7 6.3 copy-start.3
  303.6 9.6 %copy-start = (f32[128,8,8,128]{3,2,1,0:T(8,128)S(1)}, f32[128,8,8,128]{3,2,1,0:T(8,128)}, u32[]{:S(2)}) copy-start(f32[128,8,8,128]{3,2,1,0:T(8,128)} %copy.241) | copy-start | bytes 12582916 | tf_op jit(solution)/shard_map/while
  318.2 9.3 %copy-start.3 = (f32[18,128,256]{1,2,0:T(8,128)}, f32[18,128,256]{1,2,0:T(8,128)S(1)}, u32[]{:S(2)}) copy-start(f32[18,128,256]{1,2,0:T(8,128)S(1)} %add_dynamic-update-slice_fusion.5) | copy-start | bytes 7077892 | tf_op jit(solution)/shard_map/while
  350.2 9.6 %copy-start = (f32[128,8,8,128]{3,2,1,0:T(8,128)S(1)}, f32[128,8,8,128]{3,2,1,0:T(8,128)}, u32[]{:S(2)}) copy-start(f32[128,8,8,128]{3,2,1,0:T(8,128)} %copy.241) | copy-start | bytes 12582916 | tf_op jit(solution)/shard_map/while
  364.8 9.3 %copy-start.3 = (f32[18,128,256]{1,2,0:T(8,128)}, f32[18,128,256]{1,2,0:T(8,128)S(1)}, u32[]{:S(2)}) copy-start(f32[18,128,256]{1,2,0:T(8,128)S(1)} %add_dynamic-update-slice_fusion.5) | copy-start | bytes 7077892 | tf_op jit(solution)/shard_map/while
  396.7 9.6 %copy-start = (f32[128,8,8,128]{3,2,1,0:T(8,128)S(1)}, f32[128,8,8,128]{3,2,1,0:T(8,128)}, u32[]{:S(2)}) copy-start(f32[128,8,8,128]{3,2,1,0:T(8,128)} %copy.241) | copy-start | bytes 12582916 | tf_op jit(solution)/shard_map/while
  411.4 9.3 %copy-start.3 = (f32[18,128,256]{1,2,0:T(8,128)}, f32[18,128,256]{1,2,0:T(8,128)S(1)}, u32[]{:S(2)}) copy-start(f32[18,128,256]{1,2,0:T(8,128)S(1)} %add_dynamic-update-slice_fusion.5) | copy-start | bytes 7077892 | tf_op jit(solution)/shard_map/while
  432.3 8.4 %copy-start.9 = (s32[2]{0:T(128)S(1)}, s32[2]{0:T(128)}, u32[]{:S(2)}) copy-start(s32[2]{0:T(128)} %param.23) | copy-start | bytes 28
  432.3 8.4 %copy-start.4 = (f32[18,128,256]{1,2,0:T(8,128)S(1)}, f32[18,128,256]{1,2,0:T(8,128)}, u32[]{:S(2)}) copy-start(f32[18,128,256]{1,2,0:T(8,128)} %get-tuple-element.283) | copy-start | bytes 7077892
  432.3 136.5 %all-to-all-start.2 = ((bf16[64,128,256]{2,1,0:T(8,128)(2,1)}), bf16[64,128,256]{2,1,0:T(8,128)(2,1)}, u32[]{:S(2)}, u32[]{:S(2)}) async-start(bf16[64,128,256]{2,1,0:T(8,128)(2,1)} %copy.223), calls=%async_computation.2 | async-start | bytes 8388608 | tf_op jit(solution)/shard_map/all_to_all | solution.py:206
  440.7 203.5 %all-reduce.5.cloned.1.call-start = ((), (), s32[]{:S(2)}) async-start(), calls=%async_computation.3 | async-start | bytes 2097152 | tf_op jit(solution)/shard_map/psum | solution.py:212
  444.6 9.1 %collective-permute-start.2 = (bf16[128,256]{1,0:T(8,128)(2,1)S(1)}, bf16[128,256]{1,0:T(8,128)(2,1)S(1)}, u32[]{:S(2)}, u32[]{:S(2)}) collective-permute-start(bf16[128,256]{1,0:T(8,128)(2,1)S(1)} %get-tuple-element.424), channel_id=1, source_target_pairs={{4,0},{8,4},{12,8},{16,12},{20,16},{24,20},{28,24},{32,28},{36,32}... | collective-permute-start | bytes 196616 | tf_op jit(solution)/shard_map/ppermute | solution.py:41
  449.0 119.8 %copy-start.7 = (s32[64]{0:T(128)S(1)}, s32[64]{0:T(128)}, u32[]{:S(2)}) copy-start(s32[64]{0:T(128)} %get-tuple-element.382) | copy-start | bytes 772
  451.3 5.9 collective-permute-start.3
  (8 other events, 13.4 us)
Sparse Core Ops, SparseCore 0:
  48.5 186.3 all-reduce.6
  422.6 159.6 all-gather.2
  593.5 50.6 all-reduce.4
